TPU v7x, 128 devices: a whole 4x4x4 slice. The times are simulated.
128 devices in a mesh: blk: 4 (over x), tok: 32 (over y, z, core).
Axes of the slice: x: 4, y: 4, z: 4, core: 2. Of those that a mesh axis runs over, the one named last changes fastest.
Arguments:
- tokens: bfloat16 [32, 1024, 1664], P('tok', 'blk'), may hold values from -6 to 6
- segment_ids: int32 [32, 1024], P('tok'), may hold values from 0 to 31, as said below
- merge_index: int32 [32, 256, 4], P('tok'), may hold values from 0 to 1023, as said below
- segment_owner: int32 [32, 32], P('tok'), may hold values from 0 to 31, each once within a row
- ln1_gain: float32 [1664], replicated, may hold values from 0.1 to 1.9
- ln1_bias: float32 [1664], replicated, may hold values from -4 to 4
- w_qkv: bfloat16 [3, 1664, 1664], P(None, 'tok', 'blk'), may hold values from -0.15625 to 0.15625
- qkv_bias: float32 [3, 1664], P(None, 'blk'), may hold values from -6 to 6
- w_out: bfloat16 [1664, 1664], P('blk', 'tok'), may hold values from -0.15625 to 0.15625
- out_bias: float32 [1664], replicated, may hold values from -6 to 6
- ln2_gain: float32 [1664], replicated, may hold values from 0.1 to 1.9
- ln2_bias: float32 [1664], replicated, may hold values from -4 to 4
- w_fc1: bfloat16 [1664, 8192], P(None, 'blk'), may hold values from -0.15625 to 0.15625
- fc1_bias: float32 [8192], P('blk'), may hold values from -6 to 6
- w_fc2: bfloat16 [8192, 1664], P('blk'), may hold values from -0.0625 to 0.0625
- fc2_bias: float32 [1664], replicated, may hold values from -6 to 6
- ln3_gain: float32 [1664], replicated, may hold values from 0.1 to 1.9
- ln3_bias: float32 [1664], replicated, may hold values from -4 to 4
- w_proj: bfloat16 [6656, 1664], P('tok', 'blk'), may hold values from -0.078125 to 0.078125
- proj_bias: float32 [1664], P('blk'), may hold values from -6 to 6
Outputs:
- returned: bfloat16 [32, 32, 16, 1664], P('tok', None, None, 'blk')
Inputs may be any that keep to these rules, and one draw needn't show every extreme that they name: `segment_ids`: within a block each segment holds 4 to 64 tokens, one exactly 64; the four tokens of one row of merge_index share a segment. `merge_index`: the rows of one block name each token of the block exactly once. `segment_owner`: each block's row is a permutation of the owners.
All inputs are finite; a program needn't handle non-finite values.
Results may differ from a plain program's by a relative error of at most 0.015.
Values may be sent and summed in bfloat16 or wider, within the bound.
A program may use at most 128 MiB of HBM per device.

v0:
```python
import math
import jax
import jax.numpy as jnp
from jax import lax
from jax.sharding import PartitionSpec as P

HD = 104
EPS = 1e-06


def layer_norm(input_tensors, scales, offset):
    input_tensors = input_tensors.astype(jnp.float32)
    center = input_tensors - jnp.mean(input_tensors, axis=-1, keepdims=True)
    spread = jnp.mean(center * center, axis=-1, keepdims=True)
    return center * lax.rsqrt(spread + EPS) * scales + offset


def body(
    tokens,
    segment_ids,
    merge_index,
    segment_owner,
    ln1_gain,
    ln1_bias,
    w_qkv,
    qkv_bias,
    w_out,
    out_bias,
    ln2_gain,
    ln2_bias,
    w_fc1,
    fc1_bias,
    w_fc2,
    fc2_bias,
    ln3_gain,
    ln3_bias,
    w_proj,
    proj_bias,
):
    tok_block = tokens[0]
    row_count = tok_block.shape[0]
    model_width = tok_block.shape[1]
    head_cols = w_qkv.shape[2]
    heads_here = head_cols // HD
    normed_one = layer_norm(tok_block, ln1_gain, ln1_bias).astype(jnp.bfloat16)
    normed_all = lax.all_gather(normed_one, "blk", axis=0, tiled=True)
    all_rows = normed_all.shape[0]
    columns = normed_all
    projected_qkv = jnp.einsum(
        "td,cde->cte",
        columns,
        lax.all_gather(w_qkv, "tok", axis=1, tiled=True),
        preferred_element_type=jnp.float32,
    )
    projected_qkv = (projected_qkv + qkv_bias[:, None, :]).astype(jnp.bfloat16)
    projected_qkv = projected_qkv.reshape(3, all_rows, heads_here, HD)
    key_rows = projected_qkv[1]
    values = projected_qkv[2]
    segment_row = segment_ids[0]
    q_block = min(512, all_rows)
    block_count = all_rows // q_block
    query_rows = projected_qkv[0].reshape(block_count, q_block, heads_here, HD)
    query_segs = segment_row.reshape(block_count, q_block)
    score_scale = 1.0 / math.sqrt(HD)

    def attend(input_tensors):
        query_part, query_seg = input_tensors
        scores = (
            jnp.einsum("qhe,khe->hqk", query_part, key_rows, preferred_element_type=jnp.float32)
            * score_scale
        )
        allowed = query_seg[:, None] == segment_row[None, :]
        weights = jnp.where(allowed[None], jnp.exp(scores), 0.0)
        attn_probs = (weights / jnp.sum(weights, axis=-1, keepdims=True)).astype(jnp.bfloat16)
        mixed = jnp.einsum("hqk,khe->qhe", attn_probs, values, preferred_element_type=jnp.float32)
        return mixed.astype(jnp.bfloat16)

    attended = lax.map(attend, (query_rows, query_segs)).reshape(all_rows, head_cols)
    out_full = lax.all_gather(w_out, "tok", axis=1, tiled=True)
    attn_rows = lax.psum_scatter(
        jnp.dot(attended, out_full, preferred_element_type=jnp.float32).astype(jnp.bfloat16),
        "blk",
        scatter_dimension=0,
        tiled=True,
    ).astype(jnp.float32)
    after_attn = tok_block.astype(jnp.float32) + attn_rows + out_bias
    normed_two = layer_norm(after_attn, ln2_gain, ln2_bias).astype(jnp.bfloat16)
    pre_act = (
        jnp.dot(
            lax.all_gather(normed_two, "blk", axis=0, tiled=True),
            w_fc1,
            preferred_element_type=jnp.float32,
        )
        + fc1_bias
    )
    hidden_act = jax.nn.gelu(pre_act, approximate=False).astype(jnp.bfloat16)
    partial_sum = jnp.dot(hidden_act, w_fc2, preferred_element_type=jnp.float32)
    own_start = lax.axis_index("blk") * row_count
    own_rows = lax.dynamic_slice_in_dim(partial_sum, own_start, row_count, 0) + after_attn
    partial_sum = lax.dynamic_update_slice_in_dim(partial_sum, own_rows, own_start, 0)
    summed = lax.psum(partial_sum.astype(jnp.bfloat16), "blk").astype(jnp.float32)
    layer_all = (summed + fc2_bias).astype(jnp.bfloat16)
    final_all = layer_norm(layer_all, ln3_gain, ln3_bias).astype(jnp.bfloat16)
    merge_rows = merge_index[0]
    merged_count = merge_rows.shape[0]
    merged = jnp.take(final_all, merge_rows.reshape(-1), axis=0).reshape(
        merged_count, 4 * model_width
    )
    columns = merged
    projected = jnp.dot(
        columns,
        lax.all_gather(w_proj, "tok", axis=0, tiled=True),
        preferred_element_type=jnp.float32,
    )
    projected = (projected + proj_bias).astype(jnp.bfloat16)
    tok_count = lax.axis_size("tok")
    slot_cap = 2 * merged_count // tok_count
    owners_here = segment_owner[0]
    seg_rows = jnp.take(segment_row, merge_rows[:, 0])
    seg_match = (
        seg_rows[:, None] == jnp.arange(owners_here.shape[0], dtype=jnp.int32)[None, :]
    ).astype(jnp.int32)
    owner_rows = jnp.sum(seg_match * owners_here[None, :], axis=1)
    segment_matches = (
        owner_rows[:, None] == jnp.arange(tok_count, dtype=jnp.int32)[None, :]
    ).astype(jnp.int32)
    before = jnp.cumsum(segment_matches, axis=0) - segment_matches
    order_in = jnp.sum(before * segment_matches, axis=1)
    target = owner_rows * slot_cap + order_in
    placed = (jnp.arange(tok_count * slot_cap, dtype=jnp.int32)[:, None] == target[None, :]).astype(
        jnp.bfloat16
    )
    outgoing = jnp.dot(placed, projected, preferred_element_type=jnp.float32).astype(jnp.bfloat16)
    outgoing = outgoing.reshape(tok_count, slot_cap, projected.shape[1])
    arrived = lax.all_to_all(outgoing, "tok", split_axis=0, concat_axis=0, tiled=True)
    return arrived[None]


def solution(mesh):
    placed = (
        P("tok", "blk", None),
        P("tok", None),
        P("tok", None, None),
        P("tok", None),
        P(),
        P(),
        P(None, "tok", "blk"),
        P(None, "blk"),
        P("blk", "tok"),
        P(),
        P(),
        P(),
        P(None, "blk"),
        P("blk"),
        P("blk", None),
        P(),
        P(),
        P(),
        P("tok", "blk"),
        P("blk"),
    )
    return jax.shard_map(
        body, mesh=mesh, in_specs=placed, out_specs=P("tok", None, None, "blk"), check_vma=False
    )
```

profile of v0, /device:TPU:1, one launch (start us, length us, event | category | flops | bytes accessed | tf_op | source)
XLA Modules:
  0.0 480.8 jit_solution(5821261523930769322)
XLA Ops:
  6.5 0.7 all-gather.15.cloned.1.call-update
  7.3 0.0 all-gather.7.cloned.1.call-start
  7.3 1.3 convert_reduce_fusion.1
  8.7 1.5 fusion.43
  10.2 2.5 fusion.46
  12.8 0.0 all-gather.9.cloned.1.call-start
  12.8 1.7 copy.32
  14.5 0.0 reduce-scatter.2.cloned.1.call-start
  14.6 0.5 broadcast.197
  15.1 1.3 reduce.6
  16.4 40.5 %all-gather.15.cloned.1.call-done = bf16[32,52,416]{2,1,0:T(8,128)(2,1)} async-done(((bf16[1,52,416]{2,1,0:T(8,128)(2,1)}), bf16[32,52,416]{2,1,0:T(8,128)(2,1)}) %all-gather.15.cloned.1.call-update) | async-done | bytes 1384464 | tf_op jit(solution)/shard_map/all_gather | solution.py:79
  56.9 2.7 reshape.179
  59.7 39.4 %all-gather.7.cloned.1.call-done = bf16[1024,1664]{1,0:T(8,128)(2,1)} async-done(((bf16[256,1664]{1,0:T(8,128)(2,1)}), bf16[1024,1664]{1,0:T(8,128)(2,1)}) %all-gather.7.cloned.1.call-update) | async-done | bytes 3407888 | tf_op jit(solution)/shard_map/all_gather | solution.py:46
  99.1 53.1 %all-gather.9.cloned.1.call-done = bf16[3,1664,416]{2,0,1:T(4,128)(2,1)} async-done(((bf16[3,52,416]{2,0,1:T(4,128)(2,1)}), bf16[3,1664,416]{2,0,1:T(4,128)(2,1)}) %all-gather.9.cloned.1.call-update) | async-done | bytes 4153360 | tf_op jit(solution)/shard_map/all_gather | solution.py:52
  152.2 9.2 %fusion.34 = bf16[3,1024,416]{1,2,0:T(8,128)(2,1)S(1)} fusion(f32[3,416]{1,0:T(4,128)S(1)} %copy-done.15, bf16[3,1664,416]{2,0,1:T(4,128)(2,1)} %all-gather.9.cloned.1.call-done, bf16[1024,1664]{1,0:T(8,128)(2,1)} %all-gather.7.cloned.1.call-done), kind=kOutput, calls=%fused_computation.53 | convolution fusion | flops 4255580160 | bytes 10122112 | tf_op jit(solution)/shard_map/td,cde->cte/dot_general | solution.py:49
  161.4 1.4 fusion.96
  162.8 0.6 reshape_squeeze.10
  163.4 1.0 copy.34
  164.4 15.8 %while.10 = (s32[]{:T(128)}, bf16[2,512,4,104]{1,3,2,0:T(8,128)(2,1)}, s32[2,512]{1,0:T(2,128)S(1)}, s32[1,1024]{1,0:T(1,128)S(1)}, bf16[2,512,4,104]{1,3,2,0:T(...) while((s32[]{:T(128)}, bf16[2,512,4,104]{1,3,2,0:T(8,128)(2,1)}, ...), condition=%wide.region_8.9_spmd, body=%wide.region_6.8_spmd.sunk | while | flops 887830528 | bytes 31156912 | solution.py:78
  164.4 0.4 broadcast_compare_fusion.2
  164.8 4.0 fusion.112
  168.8 2.5 fusion.113
  171.3 0.9 copy-done.6
  172.3 0.4 broadcast_compare_fusion.2
  172.6 4.0 fusion.112
  176.6 2.5 fusion.113
  179.2 0.9 copy-done.6
  180.2 2.0 copy.35
  182.2 0.2 copy.40
  182.4 3.9 convolution_convert_fusion
  186.4 0.0 all-gather.11.cloned.1.call-start
  186.4 38.9 %reduce-scatter.2.cloned.1.call-done = bf16[256,1664]{1,0:T(8,128)(2,1)} async-done(((bf16[1024,1664]{1,0:T(8,128)(2,1)}), bf16[256,1664]{1,0:T(8,128)(2,1)}) %reduce-scatter.2.cloned.1.call-update) | async-done | bytes 851984 | tf_op jit(solution)/shard_map/reduce_scatter | solution.py:80
  225.3 1.5 fusion.57
  226.9 1.7 multiply_reduce_fusion
  228.5 2.6 add_convert_fusion.2
  231.2 0.0 all-reduce.2.cloned.1.call-start
  231.3 41.5 %all-gather.11.cloned.1.call-done = bf16[1024,1664]{1,0:T(8,128)(2,1)} async-done(((bf16[256,1664]{1,0:T(8,128)(2,1)}), bf16[1024,1664]{1,0:T(8,128)(2,1)}) %all-gather.11.cloned.1.call-update) | async-done | bytes 3407888 | tf_op jit(solution)/shard_map/all_gather | solution.py:90
  272.7 11.1 %fusion.97 = f32[1024,2048]{1,0:T(8,128)S(1)} fusion(bf16[1024,1664]{1,0:T(8,128)(2,1)} %all-gather.11.cloned.1.call-done, bf16[1664,2048]{1,0:T(8,128)(2,1)} %param.34), kind=kOutput, calls=%fused_computation.133 | convolution fusion | flops 6979321856 | bytes 18612224 | tf_op jit(solution)/shard_map/dot_general | solution.py:89
  283.9 28.8 %fusion.29 = f32[1024,1664]{1,0:T(8,128)S(1)} fusion(bf16[2048,1664]{1,0:T(8,128)(2,1)} %param.36, f32[1024,2048]{1,0:T(8,128)S(1)} %fusion.97, f32[2048]{0:T(1024)S(1)} %copy-done.16), kind=kOutput, calls=%fused_computation.48 | convolution fusion | flops 7117733888 | bytes 22028288 | tf_op jit(solution)/shard_map/dot_general | solution.py:97
  312.8 0.4 add_dynamic-update-slice_fusion
  313.2 2.2 convert_element_type.78
  315.4 0.0 all-gather.13.cloned.1.call-start
  315.5 0.7 all-gather.13.cloned.1.call-update
  316.2 0.1 copy.36
  316.4 0.1 reshape_squeeze.11
  316.5 1.4 gather_fusion
  317.9 0.1 select_reduce_fusion
  318.0 0.6 reduce-window.6
  318.6 0.2 slice_reduce_fusion
  318.8 0.2 copy.31
  319.0 0.9 broadcast_in_dim.40
  320.0 2.0 copy.39
  322.0 0.1 fusion.62
  322.1 73.7 %all-reduce.2.cloned.1.call-done = bf16[1024,1664]{1,0:T(8,128)(2,1)} async-done(((bf16[1024,1664]{1,0:T(8,128)(2,1)}), bf16[1024,1664]{1,0:T(8,128)(2,1)}) %all-reduce.2.cloned.1.call-update) | async-done | bytes 3407888 | tf_op jit(solution)/shard_map/psum | solution.py:101
  395.8 2.8 convert_reduce_fusion
  398.7 3.2 fusion.23
  401.9 1.8 fusion.26
  403.7 5.9 %gather_fusion.1 = bf16[1024,1664]{1,0:T(8,128)(2,1)} fusion(bf16[1024,1664]{1,0:T(8,128)(2,1)S(1)} %fusion.26, s32[1024]{0:T(1024)S(1)} %broadcast_clamp_fusion), kind=kCustom, calls=%fused_computation.1 | custom fusion | bytes 6819840 | tf_op jit(solution)/shard_map/jit(_take)/gather | solution.py:106
  409.6 5.4 %gather.15 = bf16[256,6656]{1,0:T(8,128)(2,1)S(1)} reshape(bf16[1024,1664]{1,0:T(8,128)(2,1)} %gather_fusion.1) | data formatting | bytes 6815744 | tf_op jit(solution)/shard_map/jit(_take)/gather | solution.py:106
  415.0 33.5 %all-gather.13.cloned.1.call-done = bf16[6656,416]{1,0:T(8,128)(2,1)} async-done(((bf16[208,416]{1,0:T(8,128)(2,1)}), bf16[6656,416]{1,0:T(8,128)(2,1)}) %all-gather.13.cloned.1.call-update) | async-done | bytes 5537808 | tf_op jit(solution)/shard_map/all_gather | solution.py:112
  448.5 7.0 %convolution_convert_fusion.1 = bf16[512,416]{0,1:T(8,128)(2,1)} fusion(bf16[6656,416]{1,0:T(8,128)(2,1)} %all-gather.13.cloned.1.call-done, pred[256,6656]{1,0:T(8,128)(4,1)} %bitcast.118, bf16[256,6656]{1,0:T(8,128)(2,1)S(1)} %gather.15, s32[256]{0:T(256)S(1)} %multiply_add_fusion, f32[416]{0:T(512)S(1)} %copy-done.17), kind=kOutput, calls=%fused_computation.69 | convolution fusion | flops 1528987648 | bytes 11078272 | tf_op jit(solution)/shard_map/dot_general | solution.py:133
  455.5 1.2 copy.37
  456.7 16.2 %all_to_all.5 = bf16[32,16,416]{2,1,0:T(8,128)(2,1)S(1)} all-to-all(bf16[32,16,416]{2,1,0:T(8,128)(2,1)S(1)} %bitcast.116), channel_id=1, replica_groups=mesh['blk'=4,'tok'=32] {'tok'}, dimensions={0} | all-to-all | bytes 851968 | tf_op jit(solution)/shard_map/all_to_all | solution.py:135
  472.9 0.8 copy.56
  (66 shorter events, 0.3 us)
Async XLA Ops:
  6.5 145.7 %copy-start.15 = (f32[3,416]{1,0:T(4,128)S(1)}, f32[3,416]{1,0:T(4,128)}, u32[]{:S(2)}) copy-start(f32[3,416]{1,0:T(4,128)} %param.29) | copy-start | bytes 14980
  6.5 50.4 %all-gather.15.cloned.1.call-start = ((), (), s32[]{:S(2)}) async-start(), calls=%async_computation.8 | async-start | bytes 1892352 | tf_op jit(solution)/shard_map/all_gather | solution.py:79
  7.3 91.8 %all-gather.7.cloned.1.call-start = ((), (), s32[]{:S(2)}) async-start(), calls=%async_computation.2 | async-start | bytes 4259840 | tf_op jit(solution)/shard_map/all_gather | solution.py:46
  12.8 139.4 %all-gather.9.cloned.1.call-start = ((), (), s32[]{:S(2)}) async-start(), calls=%async_computation.3 | async-start | bytes 7028736 | tf_op jit(solution)/shard_map/all_gather | solution.py:52
  14.5 210.8 %reduce-scatter.2.cloned.1.call-start = ((), (), s32[]{:S(2)}) async-start(), calls=%async_computation.4 | async-start | bytes 4259840 | tf_op jit(solution)/shard_map/reduce_scatter | solution.py:80
  161.4 3.0 copy-start
  164.4 4.3 copy-start.4
  164.4 4.3 copy-start.5
  171.3 0.9 copy-start.6
  172.2 4.3 copy-start.4
  172.2 4.3 copy-start.5
  179.1 0.9 copy-start.6
  182.4 42.9 %copy-start.1 = (bf16[1,256,1664]{2,1,0:T(8,128)(2,1)S(1)}, bf16[1,256,1664]{2,1,0:T(8,128)(2,1)}, u32[]{:S(2)}) copy-start(bf16[1,256,1664]{2,1,0:T(8,128)(2,1)} %param.22) | copy-start | bytes 2555908
  182.4 42.9 %copy-start.7 = (f32[1664]{0:T(1024)S(1)}, f32[1664]{0:T(1024)}, u32[]{:S(2)}) copy-start(f32[1664]{0:T(1024)} %param.31) | copy-start | bytes 19972
  186.4 42.2 %copy-start.10 = (f32[1664]{0:T(1024)S(1)}, f32[1664]{0:T(1024)}, u32[]{:S(2)}) copy-start(f32[1664]{0:T(1024)} %param.33) | copy-start | bytes 19972
  186.4 42.2 %copy-start.11 = (f32[1664]{0:T(1024)S(1)}, f32[1664]{0:T(1024)}, u32[]{:S(2)}) copy-start(f32[1664]{0:T(1024)} %param.32) | copy-start | bytes 19972
  186.4 86.3 %all-gather.11.cloned.1.call-start = ((), (), s32[]{:S(2)}) async-start(), calls=%async_computation.5 | async-start | bytes 4259840 | tf_op jit(solution)/shard_map/all_gather | solution.py:90
  231.2 164.6 %all-reduce.2.cloned.1.call-start = ((), (), s32[]{:S(2)}) async-start(), calls=%async_computation.6 | async-start | bytes 6815744 | tf_op jit(solution)/shard_map/psum | solution.py:101
  231.2 52.6 %copy-start.16 = (f32[2048]{0:T(1024)S(1)}, f32[2048]{0:T(1024)}, u32[]{:S(2)}) copy-start(f32[2048]{0:T(1024)} %param.35) | copy-start | bytes 24580
  283.9 28.9 %copy-start.3 = (bf16[256,1664]{1,0:T(8,128)(2,1)S(1)}, bf16[256,1664]{1,0:T(8,128)(2,1)}, u32[]{:S(2)}) copy-start(bf16[256,1664]{1,0:T(8,128)(2,1)} %reduce-scatter.2.cloned.1.call-done) | copy-start | bytes 2555908
  313.2 3.0 copy-start.9
  313.2 4.7 copy-start.14
  315.4 80.4 %copy-start.8 = (f32[1664]{0:T(1024)S(1)}, f32[1664]{0:T(1024)}, u32[]{:S(2)}) copy-start(f32[1664]{0:T(1024)} %param.37) | copy-start | bytes 19972
  315.4 133.1 %all-gather.13.cloned.1.call-start = ((), (), s32[]{:S(2)}) async-start(), calls=%async_computation.7 | async-start | bytes 7028736 | tf_op jit(solution)/shard_map/all_gather | solution.py:112
  316.2 85.7 %copy-start.12 = (f32[1664]{0:T(1024)S(1)}, f32[1664]{0:T(1024)}, u32[]{:S(2)}) copy-start(f32[1664]{0:T(1024)} %param.39) | copy-start | bytes 19972
  316.2 85.6 %copy-start.13 = (f32[1664]{0:T(1024)S(1)}, f32[1664]{0:T(1024)}, u32[]{:S(2)}) copy-start(f32[1664]{0:T(1024)} %param.38) | copy-start | bytes 19972
  395.8 6.1 %copy-start.2 = (bf16[1024,1664]{1,0:T(8,128)(2,1)S(1)}, bf16[1024,1664]{1,0:T(8,128)(2,1)}, u32[]{:S(2)}) copy-start(bf16[1024,1664]{1,0:T(8,128)(2,1)} %all-reduce.2.cloned.1.call-done) | copy-start | bytes 10223620
  409.6 39.0 %copy-start.17 = (f32[416]{0:T(512)S(1)}, f32[416]{0:T(512)}, u32[]{:S(2)}) copy-start(f32[416]{0:T(512)} %param.41) | copy-start | bytes 4996
Sparse Core Ops, SparseCore 0:
  9.6 47.2 all-gather.14
  58.6 40.4 all-gather.6
  101.3 50.8 all-gather.8
  186.5 38.7 reduce-scatter.1
  231.3 41.3 all-gather.10
  315.5 80.1 all-reduce.1
  398.0 50.4 all-gather.12
where the time goes:
time: 490 us; the launch traced here: 481 us
  waiting for transfers between devices  322 us (66%)
  matrix products  73 us (15%)
  local copies, waits for them, and re-layouts  30.3 us (6%)
  other arithmetic  24.6 us (5%)
  blocking collectives  16.2 us (3%)
  between operations  14 us (3%)
    psum x1, waiting for transfers between devices, body(): lax.psum(partial_sum.astype(jnp.bfloat16), 'blk').astype(jnp.float32)  73.7 us
    all_gather x1, waiting for transfers between devices, body(): lax.all_gather(w_qkv, 'tok', axis=1, tiled=True)  53.1 us
    all_gather x1, waiting for transfers between devices, body(): lax.all_gather(normed_two, 'blk', axis=0, tiled=True)  41.5 us
    all_gather x1, waiting for transfers between devices, body(): out_full = lax.all_gather(w_out, 'tok', axis=1, tiled=True)  40.5 us
    all_gather x1, waiting for transfers between devices, body(): normed_all = lax.all_gather(normed_one, 'blk', axis=0, tiled=True)  39.4 us
    reduce_scatter x1, waiting for transfers between devices, body(): lax.psum_scatter(jnp.dot(attended, out_full, preferred_element_type=jnp.f...  38.9 us
    all_gather x1, waiting for transfers between devices, body(): lax.all_gather(w_proj, 'tok', axis=0, tiled=True)  33.5 us
    dot_general x1, matrix products, body(): partial_sum = jnp.dot(hidden_act, w_fc2, preferred_element_type=jnp.float32)  28.8 us
  transfers between devices with their start and end apart: 7, of which 7 were waited for; matrix products, arithmetic and copies ran while one was open for 8% of the time, Pallas kernels for 0%

commit v1 on v0

--- a/solution.py
+++ b/solution.py
@@ -98,7 +98,7 @@
     own_start = lax.axis_index("blk") * row_count
     own_rows = lax.dynamic_slice_in_dim(partial_sum, own_start, row_count, 0) + after_attn
     partial_sum = lax.dynamic_update_slice_in_dim(partial_sum, own_rows, own_start, 0)
-    summed = lax.psum(partial_sum.astype(jnp.bfloat16), "blk").astype(jnp.float32)
+    summed = jnp.sum(lax.all_gather(partial_sum.astype(jnp.bfloat16), "blk"), 0).astype(jnp.float32)
     layer_all = (summed + fc2_bias).astype(jnp.bfloat16)
     final_all = layer_norm(layer_all, ln3_gain, ln3_bias).astype(jnp.bfloat16)
     merge_rows = merge_index[0]

time: 490 us -> 539 us (1.10)
  waiting for transfers between devices: 322 us -> 364 us
  other arithmetic: 24.6 us -> 31 us
    all_gather x0 -> x1, waiting for transfers between devices: none -> 121 us  [body(): lax.all_gather(partial_sum.astype(jnp.bfloat16), 'blk')]
    psum x1 -> x0, waiting for transfers between devices: 73.7 us -> none  [body(): lax.psum(partial_sum.astype(jnp.bfloat16), 'blk').astype(jnp.float32)]
    reduce_sum x0 -> x1, other arithmetic: none -> 9.18 us  [body(): jnp.sum(lax.all_gather(partial_sum.astype(jnp.bfloat16), 'blk'), 0)]
    all_gather x1, waiting for transfers between devices: 33.5 us -> 27.9 us  [body(): lax.all_gather(w_proj, 'tok', axis=0, tiled=True)]
where the time goes in v1:
time: 539 us; the launch traced here: 530 us
  waiting for transfers between devices  364 us (68%)
  matrix products  73 us (14%)
  other arithmetic  31 us (6%)
  local copies, waits for them, and re-layouts  30.6 us (6%)
  blocking collectives  16.2 us (3%)
  between operations  14.3 us (3%)
    all_gather x1, waiting for transfers between devices, body(): lax.all_gather(partial_sum.astype(jnp.bfloat16), 'blk')  121 us
    all_gather x1, waiting for transfers between devices, body(): lax.all_gather(w_qkv, 'tok', axis=1, tiled=True)  53.1 us
    all_gather x1, waiting for transfers between devices, body(): lax.all_gather(normed_two, 'blk', axis=0, tiled=True)  41.5 us
    all_gather x1, waiting for transfers between devices, body(): out_full = lax.all_gather(w_out, 'tok', axis=1, tiled=True)  40.5 us
    all_gather x1, waiting for transfers between devices, body(): normed_all = lax.all_gather(normed_one, 'blk', axis=0, tiled=True)  39.4 us
    reduce_scatter x1, waiting for transfers between devices, body(): lax.psum_scatter(jnp.dot(attended, out_full, preferred_element_type=jnp.f...  38.9 us
    dot_general x1, matrix products, body(): partial_sum = jnp.dot(hidden_act, w_fc2, preferred_element_type=jnp.float32)  28.6 us
    all_gather x1, waiting for transfers between devices, body(): lax.all_gather(w_proj, 'tok', axis=0, tiled=True)  27.9 us
  transfers between devices with their start and end apart: 7, of which 7 were waited for; matrix products, arithmetic and copies ran while one was open for 8% of the time, Pallas kernels for 0%

profile of v1, /device:TPU:1, one launch (start us, length us, event | category | flops | bytes accessed | tf_op | source)
XLA Modules:
  0.0 529.6 jit_solution(2551173348352485808)
XLA Ops:
  6.5 0.7 all-gather.19.cloned.1.call-update
  7.3 1.3 convert_reduce_fusion.1
  8.7 1.5 fusion.43
  10.2 2.5 fusion.46
  12.8 0.0 all-gather.11.cloned.1.call-start
  12.8 1.7 copy.32
  14.5 0.0 reduce-scatter.2.cloned.1.call-start
  14.6 0.5 broadcast.197
  15.1 1.3 reduce.7
  16.4 40.5 %all-gather.19.cloned.1.call-done = bf16[32,52,416]{2,1,0:T(8,128)(2,1)} async-done(((bf16[1,52,416]{2,1,0:T(8,128)(2,1)}), bf16[32,52,416]{2,1,0:T(8,128)(2,1)}) %all-gather.19.cloned.1.call-update) | async-done | bytes 1384464 | tf_op jit(solution)/shard_map/all_gather | solution.py:79
  56.9 2.7 reshape.180
  59.7 39.4 %all-gather.9.cloned.1.call-done = bf16[1024,1664]{1,0:T(8,128)(2,1)} async-done(((bf16[256,1664]{1,0:T(8,128)(2,1)}), bf16[1024,1664]{1,0:T(8,128)(2,1)}) %all-gather.9.cloned.1.call-update) | async-done | bytes 3407888 | tf_op jit(solution)/shard_map/all_gather | solution.py:46
  99.1 53.1 %all-gather.11.cloned.1.call-done = bf16[3,1664,416]{2,0,1:T(4,128)(2,1)} async-done(((bf16[3,52,416]{2,0,1:T(4,128)(2,1)}), bf16[3,1664,416]{2,0,1:T(4,128)(2,1)}) %all-gather.11.cloned.1.call-update) | async-done | bytes 4153360 | tf_op jit(solution)/shard_map/all_gather | solution.py:52
  152.2 9.2 %fusion.34 = bf16[3,1024,416]{1,2,0:T(8,128)(2,1)S(1)} fusion(f32[3,416]{1,0:T(4,128)S(1)} %copy-done.15, bf16[3,1664,416]{2,0,1:T(4,128)(2,1)} %all-gather.11.cloned.1.call-done, bf16[1024,1664]{1,0:T(8,128)(2,1)} %all-gather.9.cloned.1.call-done), kind=kOutput, calls=%fused_computation.53 | convolution fusion | flops 4255580160 | bytes 10122112 | tf_op jit(solution)/shard_map/td,cde->cte/dot_general | solution.py:49
  161.4 1.4 fusion.96
  162.8 0.6 reshape_squeeze.10
  163.4 1.0 copy.34
  164.4 15.8 %while.10 = (s32[]{:T(128)}, bf16[2,512,4,104]{1,3,2,0:T(8,128)(2,1)}, s32[2,512]{1,0:T(2,128)S(1)}, s32[1,1024]{1,0:T(1,128)S(1)}, bf16[2,512,4,104]{1,3,2,0:T(...) while((s32[]{:T(128)}, bf16[2,512,4,104]{1,3,2,0:T(8,128)(2,1)}, ...), condition=%wide.region_8.9_spmd, body=%wide.region_6.8_spmd.sunk | while | flops 887830528 | bytes 31156912 | solution.py:78
  164.4 0.4 broadcast_compare_fusion.2
  164.8 3.9 fusion.112
  168.8 2.5 fusion.113
  171.3 0.9 copy-done.6
  172.3 0.4 broadcast_compare_fusion.2
  172.6 4.0 fusion.112
  176.6 2.5 fusion.113
  179.1 0.9 copy-done.6
  180.2 2.0 copy.35
  182.3 0.2 copy.40
  182.5 3.9 convolution_convert_fusion
  186.4 0.0 all-gather.13.cloned.1.call-start
  186.5 38.9 %reduce-scatter.2.cloned.1.call-done = bf16[256,1664]{1,0:T(8,128)(2,1)} async-done(((bf16[1024,1664]{1,0:T(8,128)(2,1)}), bf16[256,1664]{1,0:T(8,128)(2,1)}) %reduce-scatter.2.cloned.1.call-update) | async-done | bytes 851984 | tf_op jit(solution)/shard_map/reduce_scatter | solution.py:80
  225.4 1.5 fusion.57
  226.9 1.7 multiply_reduce_fusion
  228.6 2.6 add_convert_fusion.2
  231.2 0.0 all-gather.17.cloned.1.call-start
  231.3 41.5 %all-gather.13.cloned.1.call-done = bf16[1024,1664]{1,0:T(8,128)(2,1)} async-done(((bf16[256,1664]{1,0:T(8,128)(2,1)}), bf16[1024,1664]{1,0:T(8,128)(2,1)}) %all-gather.13.cloned.1.call-update) | async-done | bytes 3407888 | tf_op jit(solution)/shard_map/all_gather | solution.py:90
  272.8 11.3 %fusion.97 = f32[1024,2048]{1,0:T(8,128)S(1)} fusion(bf16[1024,1664]{1,0:T(8,128)(2,1)} %all-gather.13.cloned.1.call-done, bf16[1664,2048]{1,0:T(8,128)(2,1)} %param.34), kind=kOutput, calls=%fused_computation.133 | convolution fusion | flops 6979321856 | bytes 18612224 | tf_op jit(solution)/shard_map/dot_general | solution.py:89
  284.1 28.6 %fusion.29 = f32[1024,1664]{1,0:T(8,128)S(1)} fusion(bf16[2048,1664]{1,0:T(8,128)(2,1)} %param.36, f32[1024,2048]{1,0:T(8,128)S(1)} %fusion.97, f32[2048]{0:T(1024)S(1)} %copy-done.16), kind=kOutput, calls=%fused_computation.48 | convolution fusion | flops 7117733888 | bytes 22028288 | tf_op jit(solution)/shard_map/dot_general | solution.py:97
  312.8 0.4 add_dynamic-update-slice_fusion
  313.3 2.1 convert_element_type.80
  315.4 0.0 all-gather.15.cloned.1.call-start
  315.4 0.7 all-gather.15.cloned.1.call-update
  316.2 0.1 copy.36
  316.3 0.1 reshape_squeeze.11
  316.4 1.4 gather_fusion
  317.8 0.1 select_reduce_fusion
  317.9 0.6 reduce-window.6
  318.5 0.2 slice_reduce_fusion
  318.8 0.2 copy.31
  319.0 0.9 broadcast_in_dim.40
  319.9 2.1 copy.39
  322.0 0.1 fusion.62
  322.1 121.1 %all-gather.17.cloned.1.call-done = bf16[4096,1664]{1,0:T(8,128)(2,1)} async-done(((bf16[1024,1664]{1,0:T(8,128)(2,1)}), bf16[4096,1664]{1,0:T(8,128)(2,1)}) %all-gather.17.cloned.1.call-update) | async-done | bytes 13631504 | tf_op jit(solution)/shard_map/all_gather | solution.py:101
  443.3 9.2 %reduce_sum.99 = bf16[1024,1664]{1,0:T(8,128)(2,1)S(1)} reduce(bf16[4,1024,1664]{2,1,0:T(8,128)(2,1)} %bitcast.115, bf16[]{:T(256)} %constant.57.clone.1), dimensions={0}, to_apply=%region_12.13 | reduce | flops 5111808 | bytes 17039362 | tf_op jit(solution)/shard_map/reduce_sum | solution.py:101
  452.5 0.7 convert_reduce_fusion
  453.2 1.2 fusion.23
  454.5 3.2 fusion.26
  457.7 5.8 %gather_fusion.1 = bf16[1024,1664]{1,0:T(8,128)(2,1)} fusion(bf16[1024,1664]{1,0:T(8,128)(2,1)S(1)} %fusion.26, s32[1024]{0:T(1024)S(1)} %broadcast_clamp_fusion), kind=kCustom, calls=%fused_computation.1 | custom fusion | bytes 6819840 | tf_op jit(solution)/shard_map/jit(_take)/gather | solution.py:106
  463.5 5.7 %gather.15 = bf16[256,6656]{1,0:T(8,128)(2,1)S(1)} reshape(bf16[1024,1664]{1,0:T(8,128)(2,1)} %gather_fusion.1) | data formatting | bytes 6815744 | tf_op jit(solution)/shard_map/jit(_take)/gather | solution.py:106
  469.2 27.9 %all-gather.15.cloned.1.call-done = bf16[6656,416]{1,0:T(8,128)(2,1)} async-done(((bf16[208,416]{1,0:T(8,128)(2,1)}), bf16[6656,416]{1,0:T(8,128)(2,1)}) %all-gather.15.cloned.1.call-update) | async-done | bytes 5537808 | tf_op jit(solution)/shard_map/all_gather | solution.py:112
  497.1 7.0 %convolution_convert_fusion.1 = bf16[512,416]{0,1:T(8,128)(2,1)} fusion(bf16[6656,416]{1,0:T(8,128)(2,1)} %all-gather.15.cloned.1.call-done, pred[256,6656]{1,0:T(8,128)(4,1)} %bitcast.120, bf16[256,6656]{1,0:T(8,128)(2,1)S(1)} %gather.15, s32[256]{0:T(256)S(1)} %multiply_add_fusion, f32[416]{0:T(512)S(1)} %copy-done.17), kind=kOutput, calls=%fused_computation.69 | convolution fusion | flops 1528987648 | bytes 11078272 | tf_op jit(solution)/shard_map/dot_general | solution.py:133
  504.1 1.2 copy.37
  505.3 16.2 %all_to_all.5 = bf16[32,16,416]{2,1,0:T(8,128)(2,1)S(1)} all-to-all(bf16[32,16,416]{2,1,0:T(8,128)(2,1)S(1)} %bitcast.118), channel_id=1, replica_groups=mesh['blk'=4,'tok'=32] {'tok'}, dimensions={0} | all-to-all | bytes 851968 | tf_op jit(solution)/shard_map/all_to_all | solution.py:135
  521.5 0.8 copy.55
  (67 shorter events, 0.4 us)
Async XLA Ops:
  6.5 145.7 %copy-start.15 = (f32[3,416]{1,0:T(4,128)S(1)}, f32[3,416]{1,0:T(4,128)}, u32[]{:S(2)}) copy-start(f32[3,416]{1,0:T(4,128)} %param.29) | copy-start | bytes 14980
  6.5 50.4 %all-gather.19.cloned.1.call-start = ((), (), s32[]{:S(2)}) async-start(), calls=%async_computation.8 | async-start | bytes 1892352 | tf_op jit(solution)/shard_map/all_gather | solution.py:79
  7.3 91.8 %all-gather.9.cloned.1.call-start = ((), (), s32[]{:S(2)}) async-start(), calls=%async_computation.2 | async-start | bytes 4259840 | tf_op jit(solution)/shard_map/all_gather | solution.py:46
  12.8 139.4 %all-gather.11.cloned.1.call-start = ((), (), s32[]{:S(2)}) async-start(), calls=%async_computation.3 | async-start | bytes 7028736 | tf_op jit(solution)/shard_map/all_gather | solution.py:52
  14.5 210.8 %reduce-scatter.2.cloned.1.call-start = ((), (), s32[]{:S(2)}) async-start(), calls=%async_computation.4 | async-start | bytes 4259840 | tf_op jit(solution)/shard_map/reduce_scatter | solution.py:80
  161.4 3.0 copy-start
  164.4 4.3 copy-start.4
  164.4 4.3 copy-start.5
  171.3 0.9 copy-start.6
  172.2 4.3 copy-start.4
  172.2 4.3 copy-start.5
  179.1 0.9 copy-start.6
  182.5 42.9 %copy-start.2 = (bf16[1,256,1664]{2,1,0:T(8,128)(2,1)S(1)}, bf16[1,256,1664]{2,1,0:T(8,128)(2,1)}, u32[]{:S(2)}) copy-start(bf16[1,256,1664]{2,1,0:T(8,128)(2,1)} %param.22) | copy-start | bytes 2555908
  182.5 42.9 %copy-start.7 = (f32[1664]{0:T(1024)S(1)}, f32[1664]{0:T(1024)}, u32[]{:S(2)}) copy-start(f32[1664]{0:T(1024)} %param.31) | copy-start | bytes 19972
  186.4 42.2 %copy-start.10 = (f32[1664]{0:T(1024)S(1)}, f32[1664]{0:T(1024)}, u32[]{:S(2)}) copy-start(f32[1664]{0:T(1024)} %param.33) | copy-start | bytes 19972
  186.4 42.2 %copy-start.11 = (f32[1664]{0:T(1024)S(1)}, f32[1664]{0:T(1024)}, u32[]{:S(2)}) copy-start(f32[1664]{0:T(1024)} %param.32) | copy-start | bytes 19972
  186.4 86.3 %all-gather.13.cloned.1.call-start = ((), (), s32[]{:S(2)}) async-start(), calls=%async_computation.5 | async-start | bytes 4259840 | tf_op jit(solution)/shard_map/all_gather | solution.py:90
  231.2 212.0 %all-gather.17.cloned.1.call-start = ((), (), s32[]{:S(2)}) async-start(), calls=%async_computation.7 | async-start | bytes 17039360 | tf_op jit(solution)/shard_map/all_gather | solution.py:101
  231.3 52.8 %copy-start.16 = (f32[2048]{0:T(1024)S(1)}, f32[2048]{0:T(1024)}, u32[]{:S(2)}) copy-start(f32[2048]{0:T(1024)} %param.35) | copy-start | bytes 24580
  284.1 28.7 %copy-start.3 = (bf16[256,1664]{1,0:T(8,128)(2,1)S(1)}, bf16[256,1664]{1,0:T(8,128)(2,1)}, u32[]{:S(2)}) copy-start(bf16[256,1664]{1,0:T(8,128)(2,1)} %reduce-scatter.2.cloned.1.call-done) | copy-start | bytes 2555908
  313.2 2.9 copy-start.9
  313.3 4.6 copy-start.14
  315.4 181.7 %all-gather.15.cloned.1.call-start = ((), (), s32[]{:S(2)}) async-start(), calls=%async_computation.6 | async-start | bytes 7028736 | tf_op jit(solution)/shard_map/all_gather | solution.py:112
  443.3 9.2 %copy-start.8 = (f32[1664]{0:T(1024)S(1)}, f32[1664]{0:T(1024)}, u32[]{:S(2)}) copy-start(f32[1664]{0:T(1024)} %param.37) | copy-start | bytes 19972
  452.5 2.0 copy-start.1
  452.5 2.0 copy-start.12
  452.5 2.0 copy-start.13
  463.5 33.6 %copy-start.17 = (f32[416]{0:T(512)S(1)}, f32[416]{0:T(512)}, u32[]{:S(2)}) copy-start(f32[416]{0:T(512)} %param.41) | copy-start | bytes 4996
Sparse Core Ops, SparseCore 0:
  9.6 47.2 all-gather.18
  58.6 40.4 all-gather.8
  101.3 50.8 all-gather.10
  186.6 38.7 reduce-scatter.1
  231.3 41.3 all-gather.12
  315.5 127.6 all-gather.16
  445.5 51.5 all-gather.14
